TPU v7x, 128 devices: a whole 4x4x4 slice. The times are simulated.
128 devices in a mesh: dp: 64 (over y_hi, z, x, core), col: 2 (over y_lo).
Axes of the slice: x: 4, y: 4 (y_hi: 2, y_lo: 2; y = y_hi * 2 + y_lo), z: 4, core: 2. Of those that a mesh axis runs over, the one named last changes fastest.
Arguments:
- tokens: bfloat16 [8192, 2048], P('dp'), may hold values from -6 to 6
- routes: int32 [8192, 8], P('dp'), may hold values from 0 to 127, all different within a row; in each aligned block of 128 rows (0 to 127, 128 to 255, ...) at most 12 rows name the same one
- probs: float32 [8192, 8], P('dp'), may hold values from 0.1 to 1
- w_gate: bfloat16 [128, 2048, 768], P('dp', None, 'col'), may hold values from -0.125 to 0.125
- w_up: bfloat16 [128, 2048, 768], P('dp', None, 'col'), may hold values from -0.125 to 0.125
- w_down: bfloat16 [128, 768, 2048], P('dp', 'col'), may hold values from -0.21875 to 0.21875
- cotangent: bfloat16 [8192, 2048], P('dp', 'col'), may hold values from -6 to 6
Outputs:
- mixed: bfloat16 [8192, 2048], P('dp', 'col')
- grad_tokens: bfloat16 [8192, 2048], P('dp', 'col')
- grad_probs: float32 [8192, 8], P('dp')
- grad_gate: bfloat16 [128, 2048, 768], P('dp', None, 'col')
- grad_up: bfloat16 [128, 2048, 768], P('dp', None, 'col')
- grad_down: bfloat16 [128, 768, 2048], P('dp', 'col')
Inputs may be any that keep to these rules, and one draw needn't show every extreme that they name: `routes`: each token names 8 different experts. Among the 128 tokens of one index of dp, no expert is named by more than 12 of them, a bound that some block reaches.
All inputs are finite; a program needn't handle non-finite values.
Results may differ from a plain program's by a relative error of at most 0.0064.
Values may be sent and summed in bfloat16 or wider, within the bound.
A program may use at most 192 MiB of HBM per device.

v0:
```python
import jax
import jax.numpy as jnp
from jax import lax
from jax.sharding import PartitionSpec as P


def body(tokens, routes, probs, w_gate, w_up, w_down, cotangent):
    tok_count, width = tokens.shape
    top_count = routes.shape[1]
    owners = lax.axis_size("dp")
    cols = lax.axis_size("col")
    local_experts = w_gate.shape[0]
    experts = local_experts * owners
    slot_cap = 3 * tok_count * top_count // (2 * experts)
    half_width = width // cols
    pair_count = tok_count * top_count
    rows_per_owner = local_experts * slot_cap
    slots = experts * slot_cap
    flat_routes = routes.reshape(-1)
    expert_ids = jnp.arange(experts, dtype=jnp.int32)
    onehot = (flat_routes[:, None] == expert_ids[None, :]).astype(jnp.int32)
    before = jnp.cumsum(onehot, axis=0) - onehot
    slot_index = jnp.sum(before * onehot, axis=1)
    flat_index = flat_routes * slot_cap + slot_index
    slot_ids = jnp.arange(slots, dtype=jnp.int32)
    match = flat_index.reshape(tok_count, top_count)[:, :, None] == slot_ids[None, None, :]
    weight = jnp.sum(jnp.where(match, probs[:, :, None], 0.0), axis=1)
    taken = jnp.any(match, axis=1)
    picker = taken.astype(jnp.bfloat16)
    weight_hi = weight.astype(jnp.bfloat16)
    weight_lo = (weight - weight_hi.astype(jnp.float32)).astype(jnp.bfloat16)
    prob_of_slot = jnp.sum(weight, axis=0)
    both = ("dp", "col")
    col_me = lax.axis_index("col")
    tok_half = lax.dynamic_slice_in_dim(tokens, col_me * half_width, half_width, axis=1)
    tok_rows = jnp.einsum("ts,td->sd", picker, tok_half, preferred_element_type=jnp.float32)
    cot_rows = jnp.einsum("ts,td->sd", picker, cotangent, preferred_element_type=jnp.float32)

    def spread(rows_half):
        return jnp.broadcast_to(
            rows_half.reshape(owners, 1, rows_per_owner, half_width),
            (owners, cols, rows_per_owner, half_width),
        ).reshape(owners * cols, rows_per_owner, half_width)

    def dispatch(sent):
        got = lax.all_to_all(sent, both, 0, 0, tiled=True)
        return got.reshape(owners, cols, rows_per_owner, half_width)

    tok_sent, cot_sent = lax.optimization_barrier(
        (
            spread(tok_rows.astype(jnp.bfloat16)),
            spread((prob_of_slot[:, None] * cot_rows).astype(jnp.bfloat16)),
        )
    )
    row_block = dispatch(tok_sent)
    d_out = dispatch(cot_sent)
    w_gate_h = w_gate.reshape(local_experts, cols, half_width, -1)
    w_up_h = w_up.reshape(local_experts, cols, half_width, -1)
    w_down_h = w_down.reshape(local_experts, w_down.shape[1], cols, half_width)
    expert_of_row = jnp.arange(rows_per_owner, dtype=jnp.int32) // slot_cap
    own = (expert_of_row[:, None] == jnp.arange(local_experts, dtype=jnp.int32)[None, :])[
        None, :, :, None
    ]

    def per_half(table):
        return jnp.broadcast_to(
            table.reshape(tok_count, owners, 1, rows_per_owner),
            (tok_count, owners, cols, rows_per_owner),
        )

    def send_back(halves):
        part = jnp.stack([h.astype(jnp.bfloat16) for h in halves], axis=1)
        got = lax.all_to_all(
            part.reshape(owners * cols, rows_per_owner, half_width), both, 0, 0, tiled=True
        )
        return got.reshape(owners, cols, rows_per_owner, half_width)

    def flat(got):
        return got.reshape(owners * cols * rows_per_owner, half_width)

    def combine(table, got):
        lhs = per_half(table).reshape(tok_count, owners * cols * rows_per_owner)
        return jnp.dot(lhs, flat(got), preferred_element_type=jnp.float32)

    def halves_of(ref, axis):
        return [
            lax.slice_in_dim(ref, j * half_width, (j + 1) * half_width, axis=axis)
            for j in range(cols)
        ]

    gate_acts = jnp.einsum(
        "scrd,lcdh->srlh", row_block, w_gate_h, preferred_element_type=jnp.float32
    )
    up_acts = jnp.einsum("scrd,lcdh->srlh", row_block, w_up_h, preferred_element_type=jnp.float32)
    gate_acts = jnp.where(own, gate_acts, 0.0)
    up_acts = jnp.where(own, up_acts, 0.0)
    sigmoid_g = jax.nn.sigmoid(gate_acts)
    silu_g = gate_acts * sigmoid_g
    hidden = (silu_g * up_acts).astype(jnp.bfloat16)
    out_halves = [
        jnp.einsum("srlh,lhd->srd", hidden, w, preferred_element_type=jnp.float32)
        for w in halves_of(w_down, 2)
    ]
    d_out, out_halves = lax.optimization_barrier((d_out, out_halves))
    got_out = send_back(out_halves)
    stacked = jnp.broadcast_to(
        jnp.stack([weight_hi, weight_lo]).reshape(2, tok_count, owners, 1, rows_per_owner),
        (2, tok_count, owners, cols, rows_per_owner),
    )
    both_parts = jnp.dot(
        stacked.reshape(2 * tok_count, owners * cols * rows_per_owner),
        flat(got_out),
        preferred_element_type=jnp.float32,
    )
    mixed = (both_parts[:tok_count] + both_parts[tok_count:]).astype(jnp.bfloat16)
    dots = lax.dot_general(
        cotangent, flat(got_out), (((1,), (1,)), ((), ())), preferred_element_type=jnp.float32
    ).reshape(tok_count, owners, cols, rows_per_owner)
    dots = jnp.sum(dots, axis=2).reshape(tok_count, 1, slots)
    prob_part = jnp.sum(jnp.where(match, dots, 0.0), axis=2)
    grad_down = (
        jnp.einsum("srlh,scrd->lhcd", hidden, d_out, preferred_element_type=jnp.float32)
        .astype(jnp.bfloat16)
        .reshape(w_down.shape)
    )
    d_hidden = jnp.einsum("scrd,lhcd->srlh", d_out, w_down_h, preferred_element_type=jnp.float32)
    d_hidden = jnp.where(own, d_hidden, 0.0)
    d_gate = (d_hidden * up_acts * sigmoid_g * (1.0 + gate_acts * (1.0 - sigmoid_g))).astype(
        jnp.bfloat16
    )
    d_up = (d_hidden * silu_g).astype(jnp.bfloat16)
    grad_gate = (
        jnp.einsum("scrd,srlh->lcdh", row_block, d_gate, preferred_element_type=jnp.float32)
        .astype(jnp.bfloat16)
        .reshape(w_gate.shape)
    )
    grad_up = (
        jnp.einsum("scrd,srlh->lcdh", row_block, d_up, preferred_element_type=jnp.float32)
        .astype(jnp.bfloat16)
        .reshape(w_up.shape)
    )
    got_grad = send_back(
        [
            jnp.einsum("srlh,ldh->srd", d_gate, wg, preferred_element_type=jnp.float32)
            + jnp.einsum("srlh,ldh->srd", d_up, wu, preferred_element_type=jnp.float32)
            for wg, wu in zip(halves_of(w_gate, 1), halves_of(w_up, 1))
        ]
    )
    grad_tokens = combine(picker, got_grad).astype(jnp.bfloat16)
    prob_part, mixed = lax.optimization_barrier((prob_part, mixed))
    grad_probs = lax.psum(prob_part, "col")
    return (mixed, grad_tokens, grad_probs, grad_gate, grad_up, grad_down)


def solution(mesh):
    return jax.shard_map(
        body,
        mesh=mesh,
        in_specs=(
            P("dp", None),
            P("dp", None),
            P("dp", None),
            P("dp", None, "col"),
            P("dp", None, "col"),
            P("dp", "col", None),
            P("dp", "col"),
        ),
        out_specs=(
            P("dp", "col"),
            P("dp", "col"),
            P("dp", None),
            P("dp", None, "col"),
            P("dp", None, "col"),
            P("dp", "col", None),
        ),
        check_vma=False,
    )
```

profile of v0, /device:TPU:82, one launch (start us, length us, event | category | flops | bytes accessed | tf_op | source)
XLA Modules:
  0.0 381.2 jit_solution(2753015450887470145)
XLA Ops:
  0.7 0.8 copy.69
  1.8 0.8 copy.75
  3.0 0.4 fusion.54
  3.7 3.1 fusion.11
  6.8 2.5 select_reduce_fusion
  9.3 1.0 convolution_convert_fusion
  10.3 1.0 multiply_convert_fusion
  11.4 3.4 broadcast_in_dim.86
  14.8 0.9 broadcast_in_dim.82
  15.8 80.2 %all_to_all.20 = bf16[128,24,1024]{2,1,0:T(8,128)(2,1)} all-to-all(bf16[128,24,1024]{2,1,0:T(8,128)(2,1)S(1)} %bitcast.215), channel_id=1, replica_groups=mesh['dp'=64,'col'=2] {'dp','col'}, dimensions={0} | all-to-all | bytes 12582912 | tf_op jit(solution)/shard_map/all_to_all | solution.py:46
  95.9 11.4 %all-to-all-start = ((bf16[128,24,1024]{2,1,0:T(8,128)(2,1)}), bf16[128,24,1024]{2,1,0:T(8,128)(2,1)}, u32[]{:S(2)}, u32[]{:S(2)}) async-start(bf16[128,24,1024]{2,1,0:T(8,128)(2,1)} %bitcast.212), calls=%async_computation | async-start | bytes 12582912 | tf_op jit(solution)/shard_map/all_to_all | solution.py:46
  107.4 0.9 copy.80
  108.4 0.3 copy.78
  108.8 1.7 copy.79
  110.6 7.7 %fusion.60 = f32[64,24,2,384,1]{3,1,4,2,0:T(8,128)S(1)} fusion(bf16[64,2,24,1024,1]{3,2,1,4,0:T(8,128)(2,1)} %bitcast.221, bf16[2,2,1024,384,1]{3,2,1,0,4:T(8,128)(2,1)S(1)} %bitcast.238), kind=kOutput, calls=%fused_computation.88 | convolution fusion | flops 4831838208 | bytes 14155776 | tf_op jit(solution)/shard_map/scrd,lcdh->srlh/dot_general | solution.py:91
  118.4 7.4 %multiply_convert_fusion.3 = (bf16[64,24,2,384]{3,1,2,0:T(8,128)(2,1)S(1)}, f32[64,24,2,384,1]{3,1,4,2,0:T(8,128)}) fusion(pred[24,2]{0,1:T(4,128)(4,1)S(1)} %iota_compare_fusion.4, f32[64,24,2,384,1]{3,1,4,2,0:T(8,128)S(1)} %fusion.60, bf16[64,2,24,1024,1]{3,2,1,4,0:T(8,128)(2,1)S(1)} %bitcast.225, bf16[2,2,1024,384,1]{3,2,1,0,4:T(8,128)(2,1)S(1)} %bitcast.239), kind=kOutput, calls=%fused_computation.31 | convolution fusion | flops 4841275392 | bytes 21233712 | tf_op jit(solution)/shard_map/scrd,lcdh->srlh/dot_general | solution.py:94
  125.8 4.0 %convolution_bitcast_fusion = bf16[64,24,1024]{2,1,0:T(8,128)(2,1)} fusion(bf16[64,24,2,384]{3,1,2,0:T(8,128)(2,1)S(1)} %get-tuple-element.44, bf16[2,384,2048]{2,1,0:T(8,128)(2,1)S(1)} %copy-done.8), kind=kOutput, calls=%fused_computation.43 | convolution fusion | flops 2415919104 | bytes 7077888 | tf_op jit(solution)/shard_map/srlh,lhd->srd/dot_general | solution.py:101
  129.8 4.0 %convolution_bitcast_fusion.1 = bf16[64,24,1024]{2,1,0:T(8,128)(2,1)} fusion(bf16[64,24,2,384]{3,1,2,0:T(8,128)(2,1)S(1)} %get-tuple-element.44, bf16[2,384,2048]{2,1,0:T(8,128)(2,1)S(1)} %copy-done.8), kind=kOutput, calls=%fused_computation.44 | convolution fusion | flops 2415919104 | bytes 7077888 | tf_op jit(solution)/shard_map/srlh,lhd->srd/dot_general | solution.py:101
  133.8 52.4 %all-to-all-done = bf16[128,24,1024]{2,1,0:T(8,128)(2,1)} async-done(((bf16[128,24,1024]{2,1,0:T(8,128)(2,1)}), bf16[128,24,1024]{2,1,0:T(8,128)(2,1)}, u32[]{:S(2)}, u32[]{:S(2)}) %all-to-all-start) | async-done | bytes 6291488 | tf_op jit(solution)/shard_map/all_to_all | solution.py:46
  186.2 3.4 pad_maximum_fusion
  189.6 3.3 copy.76
  192.9 10.1 %all-to-all-start.2 = ((bf16[128,24,1024]{2,1,0:T(8,128)(2,1)}), bf16[128,24,1024]{2,1,0:T(8,128)(2,1)}, u32[]{:S(2)}, u32[]{:S(2)}) async-start(bf16[128,24,1024]{2,1,0:T(8,128)(2,1)} %bitcast.213), calls=%async_computation.2 | async-start | bytes 12582912 | tf_op jit(solution)/shard_map/all_to_all | solution.py:73
  203.0 9.3 %bitcast_convert_fusion = bf16[2,384,2,1024]{3,1,2,0:T(8,128)(2,1)} fusion(bf16[64,2,24,1024]{3,2,1,0:T(8,128)(2,1)} %bitcast.7, bf16[64,24,2,384]{3,1,2,0:T(8,128)(2,1)S(1)} %get-tuple-element.44), kind=kOutput, calls=%fused_computation.6 | convolution fusion | flops 4833411072 | bytes 11796480 | tf_op jit(solution)/shard_map/srlh,scrd->lhcd/dot_general | solution.py:122
  212.3 4.6 %copy.91 = bf16[2,384,2,1024]{1,3,2,0:T(8,128)(2,1)} copy(bf16[2,384,2,1024]{3,1,2,0:T(8,128)(2,1)} %bitcast_convert_fusion) | data formatting | bytes 6291456 | tf_op jit(solution)/shard_map/convert_element_type | solution.py:123
  216.9 4.8 %copy.93 = bf16[2,384,2048]{2,1,0:T(8,128)(2,1)} copy(bf16[2,384,2048]{1,2,0:T(8,128)(2,1)} %bitcast.217) | data formatting | bytes 6291456
  221.7 14.8 %multiply_convert_fusion.1 = (bf16[64,24,2,384]{3,1,2,0:T(8,128)(2,1)}, bf16[64,24,2,384]{3,1,2,0:T(8,128)(2,1)S(1)}) fusion(pred[24,2]{0,1:T(4,128)(4,1)S(1)} %iota_compare_fusion.4, f32[64,24,2,384,1]{3,1,4,2,0:T(8,128)} %copy-done.17, f32[64,24,2,384,1]{3,1,4,2,0:T(8,128)} %get-tuple-element.45, bf16[2,48,2,8,1024]{4,3,2,1,0:T(8,128)(2,1)} %bitcast.237, ...), kind=kOutput, calls=%fused_computation.29 | convolution fusion | flops 4850712576 | bytes 23593008 | tf_op jit(solution)/shard_map/scrd,lhcd->srlh/dot_general | solution.py:126
  236.5 1.4 copy-done.14
  237.9 6.5 %fusion.17 = bf16[2,2,1024,384]{2,3,1,0:T(8,128)(2,1)} fusion(bf16[64,2,24,1024]{3,2,1,0:T(8,128)(2,1)S(1)} %bitcast.228, bf16[64,24,2,384]{3,1,2,0:T(8,128)(2,1)S(1)} %get-tuple-element.43), kind=kOutput, calls=%fused_computation.37 | convolution fusion | flops 4833411072 | bytes 11796480 | tf_op jit(solution)/shard_map/scrd,srlh->lcdh/dot_general | solution.py:133
  244.4 5.2 %copy.85 = bf16[2,2,1024,384]{3,2,1,0:T(8,128)(2,1)} copy(bf16[2,2,1024,384]{2,3,1,0:T(8,128)(2,1)} %fusion.17) | data formatting | bytes 6291456 | tf_op jit(solution)/shard_map/convert_element_type | solution.py:134
  249.6 4.3 %fusion.39 = f32[64,24,1024,1]{2,1,3,0:T(8,128)S(1)} fusion(bf16[64,24,2,384]{3,1,2,0:T(8,128)(2,1)S(1)} %copy-done.15, bf16[2,2048,384]{2,1,0:T(8,128)(2,1)} %param.10), kind=kOutput, calls=%fused_computation.52 | convolution fusion | flops 2415919104 | bytes 10223616 | tf_op jit(solution)/shard_map/srlh,ldh->srd/dot_general | solution.py:144
  253.9 2.7 fusion.42
  256.6 3.1 fusion.16
  259.8 3.1 fusion.15
  263.0 0.6 pad_maximum_fusion.1
  263.5 3.3 copy.82
  266.8 14.9 %all-to-all-done.2 = bf16[128,24,1024]{2,1,0:T(8,128)(2,1)} async-done(((bf16[128,24,1024]{2,1,0:T(8,128)(2,1)}), bf16[128,24,1024]{2,1,0:T(8,128)(2,1)}, u32[]{:S(2)}, u32[]{:S(2)}) %all-to-all-start.2) | async-done | bytes 6291488 | tf_op jit(solution)/shard_map/all_to_all | solution.py:73
  281.7 10.0 %all-to-all-start.3 = ((bf16[128,24,1024]{2,1,0:T(8,128)(2,1)}), bf16[128,24,1024]{2,1,0:T(8,128)(2,1)}, u32[]{:S(2)}, u32[]{:S(2)}) async-start(bf16[128,24,1024]{2,1,0:T(8,128)(2,1)} %bitcast.214), calls=%async_computation.3 | async-start | bytes 12582912 | tf_op jit(solution)/shard_map/all_to_all | solution.py:73
  291.8 9.3 %fusion.18 = bf16[2,2,1024,384]{2,3,1,0:T(8,128)(2,1)} fusion(bf16[64,2,24,1024]{3,2,1,0:T(8,128)(2,1)} %bitcast.222, bf16[64,24,2,384]{3,1,2,0:T(8,128)(2,1)S(1)} %copy-done.13), kind=kOutput, calls=%fused_computation.38 | convolution fusion | flops 4833411072 | bytes 11796480 | tf_op jit(solution)/shard_map/scrd,srlh->lcdh/dot_general | solution.py:138
  301.1 4.7 %copy.88 = bf16[2,2,1024,384]{3,2,1,0:T(8,128)(2,1)} copy(bf16[2,2,1024,384]{2,3,1,0:T(8,128)(2,1)} %fusion.18) | data formatting | bytes 6291456 | tf_op jit(solution)/shard_map/convert_element_type | solution.py:139
  305.7 4.6 %fusion.61 = f32[3072,128]{1,0:T(8,128)S(1)} fusion(bf16[3072,1024]{1,0:T(8,128)(2,1)} %bitcast.30, bf16[128,1024]{1,0:T(8,128)(2,1)S(1)} %copy-done.6), kind=kOutput, calls=%fused_computation.89 | convolution fusion | flops 805306368 | bytes 8126464 | tf_op jit(solution)/shard_map/dot_general | solution.py:116
  310.5 0.3 copy.77
  310.8 1.9 broadcast_in_dim.92
  312.7 4.7 %fusion.35 = f32[256,1024]{1,0:T(8,128)S(1)} fusion(bf16[3072,1024]{1,0:T(8,128)(2,1)} %bitcast.30, bf16[384,8,2,128]{3,2,1,0:T(2,128)(2,1)S(1)} %bitcast.216), kind=kOutput, calls=%fused_computation.48 | convolution fusion | flops 1610612736 | bytes 8912896 | tf_op jit(solution)/shard_map/dot_general | solution.py:110
  317.4 0.8 fusion.52
  318.2 0.9 select_reduce_fusion.2
  319.1 56.5 %psum.7 = f32[128,8]{1,0:T(8,128)S(1)} all-reduce(f32[128,8]{1,0:T(8,128)S(1)} %select_reduce_fusion.2), channel_id=1, replica_groups=mesh['dp'=64,'col'=2] {'col'}, use_global_device_ids=true, to_apply=%region_8.9 | all-reduce | flops 1024 | bytes 8192 | tf_op jit(solution)/shard_map/psum | solution.py:151
  375.6 0.7 copy.92
  376.4 4.6 %convolution_convert_fusion.1 = bf16[128,1024]{1,0:T(8,128)(2,1)} fusion(bf16[128,3072]{0,1:T(8,128)(2,1)S(1)} %bitcast.230, bf16[3072,1024]{1,0:T(8,128)(2,1)} %bitcast.58), kind=kOutput, calls=%fused_computation.65 | convolution fusion | flops 805437440 | bytes 7340032 | tf_op jit(solution)/shard_map/dot_general | solution.py:83
  (66 shorter events, 1.5 us)
Async XLA Ops:
  0.6 8.6 %copy-start = (bf16[128,2048]{1,0:T(8,128)(2,1)S(1)}, bf16[128,2048]{1,0:T(8,128)(2,1)}, u32[]{:S(2)}) copy-start(bf16[128,2048]{1,0:T(8,128)(2,1)} %param.7) | copy-start | bytes 1572868
  0.6 2.9 copy-start.7
  2.9 7.4 %copy-start.5 = (bf16[128,1024]{1,0:T(8,128)(2,1)S(1)}, bf16[128,1024]{1,0:T(8,128)(2,1)}, u32[]{:S(2)}) copy-start(bf16[128,1024]{1,0:T(8,128)(2,1)} %param.13) | copy-start | bytes 786436
  3.6 7.7 %copy-start.3 = (s32[128,8]{1,0:T(8,128)}, s32[128,8]{1,0:T(8,128)S(1)}, u32[]{:S(2)}) copy-start(s32[128,8]{1,0:T(8,128)S(1)} %copy.74) | copy-start | bytes 12292
  95.9 90.2 %all-to-all-start = ((bf16[128,24,1024]{2,1,0:T(8,128)(2,1)}), bf16[128,24,1024]{2,1,0:T(8,128)(2,1)}, u32[]{:S(2)}, u32[]{:S(2)}) async-start(bf16[128,24,1024]{2,1,0:T(8,128)(2,1)} %bitcast.212), calls=%async_computation | async-start | bytes 12582912 | tf_op jit(solution)/shard_map/all_to_all | solution.py:46
  108.6 2.0 copy-start.9
  108.8 9.5 %slice-start = ((s8[6291456]{0:T(1024)(128)(4,1)}), s8[4194304]{0:T(1024)(128)(4,1)S(1)}, s32[]{:S(2)}) async-start(s8[6291456]{0:T(1024)(128)(4,1)} %bitcast.223), calls=%async_computation.4 | async-start | bytes 8388608
  110.6 7.7 %slice-start.1 = ((s8[6291456]{0:T(1024)(128)(4,1)}), s8[2097152]{0:T(1024)(128)(4,1)S(1)}, s32[]{:S(2)}) async-start(s8[6291456]{0:T(1024)(128)(4,1)} %bitcast.223), calls=%async_computation.5 | async-start | bytes 4194304
  110.6 7.7 %copy-start.11 = (bf16[2,2048,384]{2,1,0:T(8,128)(2,1)S(1)}, bf16[2,2048,384]{2,1,0:T(8,128)(2,1)}, u32[]{:S(2)}) copy-start(bf16[2,2048,384]{2,1,0:T(8,128)(2,1)} %param.11) | copy-start | bytes 9437188
  118.3 7.5 %copy-start.17 = (f32[64,24,2,384,1]{3,1,4,2,0:T(8,128)}, f32[64,24,2,384,1]{3,1,4,2,0:T(8,128)S(1)}, u32[]{:S(2)}) copy-start(f32[64,24,2,384,1]{3,1,4,2,0:T(8,128)S(1)} %fusion.60) | copy-start | bytes 14155780
  118.4 7.4 %copy-start.8 = (bf16[2,384,2048]{2,1,0:T(8,128)(2,1)S(1)}, bf16[2,384,2048]{2,1,0:T(8,128)(2,1)}, u32[]{:S(2)}) copy-start(bf16[2,384,2048]{2,1,0:T(8,128)(2,1)} %param.12) | copy-start | bytes 9437188
  192.9 88.8 %all-to-all-start.2 = ((bf16[128,24,1024]{2,1,0:T(8,128)(2,1)}), bf16[128,24,1024]{2,1,0:T(8,128)(2,1)}, u32[]{:S(2)}, u32[]{:S(2)}) async-start(bf16[128,24,1024]{2,1,0:T(8,128)(2,1)} %bitcast.213), calls=%async_computation.2 | async-start | bytes 12582912 | tf_op jit(solution)/shard_map/all_to_all | solution.py:73
  216.9 21.0 %slice-start.2 = ((s8[6291456]{0:T(1024)(128)(4,1)}), s8[2097152]{0:T(1024)(128)(4,1)S(1)}, s32[]{:S(2)}) async-start(s8[6291456]{0:T(1024)(128)(4,1)} %bitcast.226), calls=%async_computation.6 | async-start | bytes 4194304
  221.7 16.2 %slice-start.3 = ((s8[6291456]{0:T(1024)(128)(4,1)}), s8[4194304]{0:T(1024)(128)(4,1)S(1)}, s32[]{:S(2)}) async-start(s8[6291456]{0:T(1024)(128)(4,1)} %bitcast.226), calls=%async_computation.7 | async-start | bytes 8388608
  236.5 1.4 copy-start.14
  244.4 5.2 %copy-start.15 = (bf16[64,24,2,384]{3,1,2,0:T(8,128)(2,1)S(1)}, bf16[64,24,2,384]{3,1,2,0:T(8,128)(2,1)}, u32[]{:S(2)}) copy-start(bf16[64,24,2,384]{3,1,2,0:T(8,128)(2,1)} %copy-done.14) | copy-start | bytes 7077892
  249.6 4.3 %copy-start.10 = (bf16[2,2048,384]{2,1,0:T(8,128)(2,1)S(1)}, bf16[2,2048,384]{2,1,0:T(8,128)(2,1)}, u32[]{:S(2)}) copy-start(bf16[2,2048,384]{2,1,0:T(8,128)(2,1)} %param.10) | copy-start | bytes 9437188
  249.6 4.3 %copy-start.16 = (bf16[64,24,2,384]{3,1,2,0:T(8,128)(2,1)S(1)}, bf16[64,24,2,384]{3,1,2,0:T(8,128)(2,1)}, u32[]{:S(2)}) copy-start(bf16[64,24,2,384]{3,1,2,0:T(8,128)(2,1)} %copy-done.14) | copy-start | bytes 7077892
  253.9 2.8 copy-start.12
  253.9 2.7 copy-start.13
  281.7 94.5 %all-to-all-start.3 = ((bf16[128,24,1024]{2,1,0:T(8,128)(2,1)}), bf16[128,24,1024]{2,1,0:T(8,128)(2,1)}, u32[]{:S(2)}, u32[]{:S(2)}) async-start(bf16[128,24,1024]{2,1,0:T(8,128)(2,1)} %bitcast.214), calls=%async_computation.3 | async-start | bytes 12582912 | tf_op jit(solution)/shard_map/all_to_all | solution.py:73
  301.1 4.7 %copy-start.6 = (bf16[128,1024]{1,0:T(8,128)(2,1)S(1)}, bf16[128,1024]{1,0:T(8,128)(2,1)}, u32[]{:S(2)}) copy-start(bf16[128,1024]{1,0:T(8,128)(2,1)} %param.13) | copy-start | bytes 786436
  312.7 5.5 %copy-start.4 = (s32[128,8]{1,0:T(8,128)S(1)}, s32[128,8]{1,0:T(8,128)}, u32[]{:S(2)}) copy-start(s32[128,8]{1,0:T(8,128)} %copy-done.3) | copy-start | bytes 12292
  312.7 63.5 %copy-start.2 = (bf16[128,1536]{0,1:T(8,128)(2,1)S(1)}, bf16[128,1536]{0,1:T(8,128)(2,1)}, u32[]{:S(2)}) copy-start(bf16[128,1536]{0,1:T(8,128)(2,1)} %copy.80) | copy-start | bytes 1179652
  376.4 4.6 %copy-start.1 = (bf16[128,2048]{1,0:T(8,128)(2,1)S(1)}, bf16[128,2048]{1,0:T(8,128)(2,1)}, u32[]{:S(2)}) copy-start(bf16[128,2048]{1,0:T(8,128)(2,1)} %param.7) | copy-start | bytes 1572868
where the time goes:
time: 389 us; the launch traced here: 381 us
  blocking collectives  137 us (35%)
  matrix products  92.1 us (24%)
  waiting for transfers between devices  67.3 us (17%)
  local copies, waits for them, and re-layouts  39.9 us (10%)
  starting transfers between devices  31.5 us (8%)
  other arithmetic  12.3 us (3%)
    all_to_all x1, blocking collectives, dispatch(): got = lax.all_to_all(sent, both, 0, 0, tiled=True)  80.2 us
    psum x1, blocking collectives, body(): grad_probs = lax.psum(prob_part, 'col')  56.5 us
    all_to_all x1, waiting for transfers between devices, dispatch(): got = lax.all_to_all(sent, both, 0, 0, tiled=True)  52.4 us
    all_to_all x2, starting transfers between devices, send_back(): lax.all_to_all(part.reshape(owners * cols, rows_per_owner, half_width), b...  20.1 us
    all_to_all x2, waiting for transfers between devices, send_back(): lax.all_to_all(part.reshape(owners * cols, rows_per_owner, half_width), b...  14.9 us
    dot_general x1, matrix products, body(): jnp.einsum('scrd,lhcd->srlh', d_out, w_down_h, preferred_element_type=jnp...  14.8 us
    all_to_all x1, starting transfers between devices, dispatch(): got = lax.all_to_all(sent, both, 0, 0, tiled=True)  11.4 us
    dot_general x1, matrix products, body(): jnp.einsum('srlh,scrd->lhcd', hidden, d_out, preferred_element_type=jnp.f...  9.29 us
  transfers between devices with their start and end apart: 3, of which 2 were waited for; matrix products, arithmetic and copies ran while one was open for 31% of the time, Pallas kernels for 0%

commit v1 on v0

--- a/solution.py
+++ b/solution.py
@@ -148,7 +148,7 @@
     )
     grad_tokens = combine(picker, got_grad).astype(jnp.bfloat16)
     prob_part, mixed = lax.optimization_barrier((prob_part, mixed))
-    grad_probs = lax.psum(prob_part, "col")
+    grad_probs = jnp.sum(lax.all_gather(prob_part, "col"), axis=0)
     return (mixed, grad_tokens, grad_probs, grad_gate, grad_up, grad_down)
 
 

time: 389 us -> 387 us (level)
  the two profiles are of different devices: /device:TPU:82 before, /device:TPU:98 now
where the time goes in v1:
time: 387 us; the launch traced here: 379 us
  blocking collectives  129 us (33%)
  matrix products  92.1 us (24%)
  waiting for transfers between devices  83.4 us (22%)
  local copies, waits for them, and re-layouts  39.9 us (10%)
  starting transfers between devices  21.5 us (6%)
  other arithmetic  12.3 us (3%)
    all_to_all x1, blocking collectives, dispatch(): got = lax.all_to_all(sent, both, 0, 0, tiled=True)  82.9 us
    all_to_all x1, waiting for transfers between devices, dispatch(): got = lax.all_to_all(sent, both, 0, 0, tiled=True)  56 us
    all_gather x1, blocking collectives, body(): grad_probs = jnp.sum(lax.all_gather(prob_part, 'col'), axis=0)  45.9 us
    all_to_all x2, waiting for transfers between devices, send_back(): lax.all_to_all(part.reshape(owners * cols, rows_per_owner, half_width), b...  27.4 us
    dot_general x1, matrix products, body(): jnp.einsum('scrd,lhcd->srlh', d_out, w_down_h, preferred_element_type=jnp...  14.8 us
    all_to_all x2, starting transfers between devices, send_back(): lax.all_to_all(part.reshape(owners * cols, rows_per_owner, half_width), b...  12.9 us
    dot_general x1, matrix products, body(): jnp.einsum('srlh,scrd->lhcd', hidden, d_out, preferred_element_type=jnp.f...  9.3 us
    dot_general x1, matrix products, body(): jnp.einsum('scrd,srlh->lcdh', row_block, d_up, preferred_element_type=jnp...  9.29 us
  transfers between devices with their start and end apart: 3, of which 3 were waited for; matrix products, arithmetic and copies ran while one was open for 31% of the time, Pallas kernels for 0%

profile of v1, /device:TPU:98, one launch (start us, length us, event | category | flops | bytes accessed | tf_op | source)
XLA Modules:
  0.0 379.4 jit_solution(10619890321689972493)
XLA Ops:
  0.7 0.8 copy.69
  1.8 0.8 copy.75
  3.0 0.4 fusion.54
  3.7 3.1 fusion.11
  6.8 2.5 select_reduce_fusion
  9.3 1.0 convolution_convert_fusion
  10.3 1.0 multiply_convert_fusion
  11.4 3.4 broadcast_in_dim.86
  14.8 0.9 broadcast_in_dim.82
  15.8 82.9 %all_to_all.20 = bf16[128,24,1024]{2,1,0:T(8,128)(2,1)} all-to-all(bf16[128,24,1024]{2,1,0:T(8,128)(2,1)S(1)} %bitcast.216), channel_id=1, replica_groups=mesh['dp'=64,'col'=2] {'dp','col'}, dimensions={0} | all-to-all | bytes 12582912 | tf_op jit(solution)/shard_map/all_to_all | solution.py:46
  98.7 8.6 %all-to-all-start = ((bf16[128,24,1024]{2,1,0:T(8,128)(2,1)}), bf16[128,24,1024]{2,1,0:T(8,128)(2,1)}, u32[]{:S(2)}, u32[]{:S(2)}) async-start(bf16[128,24,1024]{2,1,0:T(8,128)(2,1)} %bitcast.214), calls=%async_computation | async-start | bytes 12582912 | tf_op jit(solution)/shard_map/all_to_all | solution.py:46
  107.3 0.9 copy.80
  108.8 1.7 copy.79
  110.5 7.7 %fusion.60 = f32[64,24,2,384,1]{3,1,4,2,0:T(8,128)S(1)} fusion(bf16[64,2,24,1024,1]{3,2,1,4,0:T(8,128)(2,1)} %bitcast.222, bf16[2,2,1024,384,1]{3,2,1,0,4:T(8,128)(2,1)S(1)} %bitcast.240), kind=kOutput, calls=%fused_computation.88 | convolution fusion | flops 4831838208 | bytes 14155776 | tf_op jit(solution)/shard_map/scrd,lcdh->srlh/dot_general | solution.py:91
  118.3 7.4 %multiply_convert_fusion.3 = (bf16[64,24,2,384]{3,1,2,0:T(8,128)(2,1)S(1)}, f32[64,24,2,384,1]{3,1,4,2,0:T(8,128)}) fusion(pred[24,2]{0,1:T(4,128)(4,1)S(1)} %iota_compare_fusion.4, f32[64,24,2,384,1]{3,1,4,2,0:T(8,128)S(1)} %fusion.60, bf16[64,2,24,1024,1]{3,2,1,4,0:T(8,128)(2,1)S(1)} %bitcast.226, bf16[2,2,1024,384,1]{3,2,1,0,4:T(8,128)(2,1)S(1)} %bitcast.241), kind=kOutput, calls=%fused_computation.31 | convolution fusion | flops 4841275392 | bytes 21233712 | tf_op jit(solution)/shard_map/scrd,lcdh->srlh/dot_general | solution.py:94
  125.7 4.0 %convolution_bitcast_fusion = bf16[64,24,1024]{2,1,0:T(8,128)(2,1)} fusion(bf16[64,24,2,384]{3,1,2,0:T(8,128)(2,1)S(1)} %get-tuple-element.44, bf16[2,384,2048]{2,1,0:T(8,128)(2,1)S(1)} %copy-done.8), kind=kOutput, calls=%fused_computation.43 | convolution fusion | flops 2415919104 | bytes 7077888 | tf_op jit(solution)/shard_map/srlh,lhd->srd/dot_general | solution.py:101
  129.7 4.0 %convolution_bitcast_fusion.1 = bf16[64,24,1024]{2,1,0:T(8,128)(2,1)} fusion(bf16[64,24,2,384]{3,1,2,0:T(8,128)(2,1)S(1)} %get-tuple-element.44, bf16[2,384,2048]{2,1,0:T(8,128)(2,1)S(1)} %copy-done.8), kind=kOutput, calls=%fused_computation.44 | convolution fusion | flops 2415919104 | bytes 7077888 | tf_op jit(solution)/shard_map/srlh,lhd->srd/dot_general | solution.py:101
  133.7 56.0 %all-to-all-done = bf16[128,24,1024]{2,1,0:T(8,128)(2,1)} async-done(((bf16[128,24,1024]{2,1,0:T(8,128)(2,1)}), bf16[128,24,1024]{2,1,0:T(8,128)(2,1)}, u32[]{:S(2)}, u32[]{:S(2)}) %all-to-all-start) | async-done | bytes 6291488 | tf_op jit(solution)/shard_map/all_to_all | solution.py:46
  189.7 3.4 pad_maximum_fusion
  193.1 3.3 copy.76
  196.4 6.5 %all-to-all-start.2 = ((bf16[128,24,1024]{2,1,0:T(8,128)(2,1)}), bf16[128,24,1024]{2,1,0:T(8,128)(2,1)}, u32[]{:S(2)}, u32[]{:S(2)}) async-start(bf16[128,24,1024]{2,1,0:T(8,128)(2,1)} %bitcast.215), calls=%async_computation.2 | async-start | bytes 12582912 | tf_op jit(solution)/shard_map/all_to_all | solution.py:73
  202.9 9.3 %bitcast_convert_fusion = bf16[2,384,2,1024]{3,1,2,0:T(8,128)(2,1)} fusion(bf16[64,2,24,1024]{3,2,1,0:T(8,128)(2,1)} %bitcast.7, bf16[64,24,2,384]{3,1,2,0:T(8,128)(2,1)S(1)} %get-tuple-element.44), kind=kOutput, calls=%fused_computation.6 | convolution fusion | flops 4833411072 | bytes 11796480 | tf_op jit(solution)/shard_map/srlh,scrd->lhcd/dot_general | solution.py:122
  212.2 4.6 %copy.92 = bf16[2,384,2,1024]{1,3,2,0:T(8,128)(2,1)} copy(bf16[2,384,2,1024]{3,1,2,0:T(8,128)(2,1)} %bitcast_convert_fusion) | data formatting | bytes 6291456 | tf_op jit(solution)/shard_map/convert_element_type | solution.py:123
  216.8 4.8 %copy.93 = bf16[2,384,2048]{2,1,0:T(8,128)(2,1)} copy(bf16[2,384,2048]{1,2,0:T(8,128)(2,1)} %bitcast.218) | data formatting | bytes 6291456
  221.6 14.8 %multiply_convert_fusion.1 = (bf16[64,24,2,384]{3,1,2,0:T(8,128)(2,1)}, bf16[64,24,2,384]{3,1,2,0:T(8,128)(2,1)S(1)}) fusion(pred[24,2]{0,1:T(4,128)(4,1)S(1)} %iota_compare_fusion.4, f32[64,24,2,384,1]{3,1,4,2,0:T(8,128)} %copy-done.17, f32[64,24,2,384,1]{3,1,4,2,0:T(8,128)} %get-tuple-element.45, bf16[2,48,2,8,1024]{4,3,2,1,0:T(8,128)(2,1)} %bitcast.239, ...), kind=kOutput, calls=%fused_computation.29 | convolution fusion | flops 4850712576 | bytes 23593008 | tf_op jit(solution)/shard_map/scrd,lhcd->srlh/dot_general | solution.py:126
  236.4 1.4 copy-done.14
  237.8 6.5 %fusion.17 = bf16[2,2,1024,384]{2,3,1,0:T(8,128)(2,1)} fusion(bf16[64,2,24,1024]{3,2,1,0:T(8,128)(2,1)S(1)} %bitcast.229, bf16[64,24,2,384]{3,1,2,0:T(8,128)(2,1)S(1)} %get-tuple-element.43), kind=kOutput, calls=%fused_computation.37 | convolution fusion | flops 4833411072 | bytes 11796480 | tf_op jit(solution)/shard_map/scrd,srlh->lcdh/dot_general | solution.py:133
  244.3 5.2 %copy.86 = bf16[2,2,1024,384]{3,2,1,0:T(8,128)(2,1)} copy(bf16[2,2,1024,384]{2,3,1,0:T(8,128)(2,1)} %fusion.17) | data formatting | bytes 6291456 | tf_op jit(solution)/shard_map/convert_element_type | solution.py:134
  249.5 4.3 %fusion.39 = f32[64,24,1024,1]{2,1,3,0:T(8,128)S(1)} fusion(bf16[64,24,2,384]{3,1,2,0:T(8,128)(2,1)S(1)} %copy-done.15, bf16[2,2048,384]{2,1,0:T(8,128)(2,1)} %param.10), kind=kOutput, calls=%fused_computation.52 | convolution fusion | flops 2415919104 | bytes 10223616 | tf_op jit(solution)/shard_map/srlh,ldh->srd/dot_general | solution.py:144
  253.8 2.7 fusion.42
  256.6 3.1 fusion.16
  259.7 3.1 fusion.15
  262.9 0.6 pad_maximum_fusion.1
  263.4 3.3 copy.82
  266.8 18.5 %all-to-all-done.2 = bf16[128,24,1024]{2,1,0:T(8,128)(2,1)} async-done(((bf16[128,24,1024]{2,1,0:T(8,128)(2,1)}), bf16[128,24,1024]{2,1,0:T(8,128)(2,1)}, u32[]{:S(2)}, u32[]{:S(2)}) %all-to-all-start.2) | async-done | bytes 6291488 | tf_op jit(solution)/shard_map/all_to_all | solution.py:73
  285.2 6.4 %all-to-all-start.3 = ((bf16[128,24,1024]{2,1,0:T(8,128)(2,1)}), bf16[128,24,1024]{2,1,0:T(8,128)(2,1)}, u32[]{:S(2)}, u32[]{:S(2)}) async-start(bf16[128,24,1024]{2,1,0:T(8,128)(2,1)} %bitcast.213), calls=%async_computation.3 | async-start | bytes 12582912 | tf_op jit(solution)/shard_map/all_to_all | solution.py:73
  291.7 9.3 %fusion.18 = bf16[2,2,1024,384]{2,3,1,0:T(8,128)(2,1)} fusion(bf16[64,2,24,1024]{3,2,1,0:T(8,128)(2,1)} %bitcast.223, bf16[64,24,2,384]{3,1,2,0:T(8,128)(2,1)S(1)} %copy-done.13), kind=kOutput, calls=%fused_computation.38 | convolution fusion | flops 4833411072 | bytes 11796480 | tf_op jit(solution)/shard_map/scrd,srlh->lcdh/dot_general | solution.py:138
  301.0 4.7 %copy.89 = bf16[2,2,1024,384]{3,2,1,0:T(8,128)(2,1)} copy(bf16[2,2,1024,384]{2,3,1,0:T(8,128)(2,1)} %fusion.18) | data formatting | bytes 6291456 | tf_op jit(solution)/shard_map/convert_element_type | solution.py:139
  305.6 4.6 %fusion.61 = f32[3072,128]{1,0:T(8,128)S(1)} fusion(bf16[3072,1024]{1,0:T(8,128)(2,1)} %bitcast.30, bf16[128,1024]{1,0:T(8,128)(2,1)S(1)} %copy-done.6), kind=kOutput, calls=%fused_computation.89 | convolution fusion | flops 805306368 | bytes 8126464 | tf_op jit(solution)/shard_map/dot_general | solution.py:116
  310.4 0.3 copy.77
  310.7 1.9 broadcast_in_dim.92
  312.6 4.7 %fusion.35 = f32[256,1024]{1,0:T(8,128)S(1)} fusion(bf16[3072,1024]{1,0:T(8,128)(2,1)} %bitcast.30, bf16[384,8,2,128]{3,2,1,0:T(2,128)(2,1)S(1)} %bitcast.217), kind=kOutput, calls=%fused_computation.48 | convolution fusion | flops 1610612736 | bytes 8912896 | tf_op jit(solution)/shard_map/dot_general | solution.py:110
  317.3 0.8 fusion.52
  318.1 0.9 select_reduce_fusion.2
  319.0 45.9 %all-gather = f32[256,8]{1,0:T(8,128)S(1)} all-gather(f32[128,8]{1,0:T(8,128)S(1)} %select_reduce_fusion.2), channel_id=2, replica_groups=mesh['dp'=64,'col'=2] {'col'}, dimensions={0}, use_global_device_ids=true | all-gather | bytes 12288 | tf_op jit(solution)/shard_map/all_gather | solution.py:151
  364.9 0.7 copy.117
  365.6 8.9 %all-to-all-done.3 = bf16[128,24,1024]{2,1,0:T(8,128)(2,1)} async-done(((bf16[128,24,1024]{2,1,0:T(8,128)(2,1)}), bf16[128,24,1024]{2,1,0:T(8,128)(2,1)}, u32[]{:S(2)}, u32[]{:S(2)}) %all-to-all-start.3) | async-done | bytes 6291488 | tf_op jit(solution)/shard_map/all_to_all | solution.py:73
  374.6 4.6 %convolution_convert_fusion.1 = bf16[128,1024]{1,0:T(8,128)(2,1)} fusion(bf16[128,3072]{0,1:T(8,128)(2,1)S(1)} %bitcast.230, bf16[3072,1024]{1,0:T(8,128)(2,1)} %bitcast.58), kind=kOutput, calls=%fused_computation.65 | convolution fusion | flops 805437440 | bytes 7340032 | tf_op jit(solution)/shard_map/dot_general | solution.py:83
  (67 shorter events, 1.8 us)
Async XLA Ops:
  0.6 8.6 %copy-start = (bf16[128,2048]{1,0:T(8,128)(2,1)S(1)}, bf16[128,2048]{1,0:T(8,128)(2,1)}, u32[]{:S(2)}) copy-start(bf16[128,2048]{1,0:T(8,128)(2,1)} %param.7) | copy-start | bytes 1572868
  0.6 2.9 copy-start.7
  2.9 7.4 %copy-start.5 = (bf16[128,1024]{1,0:T(8,128)(2,1)S(1)}, bf16[128,1024]{1,0:T(8,128)(2,1)}, u32[]{:S(2)}) copy-start(bf16[128,1024]{1,0:T(8,128)(2,1)} %param.13) | copy-start | bytes 786436
  3.6 7.7 %copy-start.3 = (s32[128,8]{1,0:T(8,128)}, s32[128,8]{1,0:T(8,128)S(1)}, u32[]{:S(2)}) copy-start(s32[128,8]{1,0:T(8,128)S(1)} %copy.74) | copy-start | bytes 12292
  98.7 91.0 %all-to-all-start = ((bf16[128,24,1024]{2,1,0:T(8,128)(2,1)}), bf16[128,24,1024]{2,1,0:T(8,128)(2,1)}, u32[]{:S(2)}, u32[]{:S(2)}) async-start(bf16[128,24,1024]{2,1,0:T(8,128)(2,1)} %bitcast.214), calls=%async_computation | async-start | bytes 12582912 | tf_op jit(solution)/shard_map/all_to_all | solution.py:46
  108.5 2.0 copy-start.9
  108.7 9.5 %slice-start = ((s8[6291456]{0:T(1024)(128)(4,1)}), s8[4194304]{0:T(1024)(128)(4,1)S(1)}, s32[]{:S(2)}) async-start(s8[6291456]{0:T(1024)(128)(4,1)} %bitcast.224), calls=%async_computation.4 | async-start | bytes 8388608
  110.5 7.7 %slice-start.1 = ((s8[6291456]{0:T(1024)(128)(4,1)}), s8[2097152]{0:T(1024)(128)(4,1)S(1)}, s32[]{:S(2)}) async-start(s8[6291456]{0:T(1024)(128)(4,1)} %bitcast.224), calls=%async_computation.5 | async-start | bytes 4194304
  110.5 7.7 %copy-start.11 = (bf16[2,2048,384]{2,1,0:T(8,128)(2,1)S(1)}, bf16[2,2048,384]{2,1,0:T(8,128)(2,1)}, u32[]{:S(2)}) copy-start(bf16[2,2048,384]{2,1,0:T(8,128)(2,1)} %param.11) | copy-start | bytes 9437188
  118.2 7.5 %copy-start.17 = (f32[64,24,2,384,1]{3,1,4,2,0:T(8,128)}, f32[64,24,2,384,1]{3,1,4,2,0:T(8,128)S(1)}, u32[]{:S(2)}) copy-start(f32[64,24,2,384,1]{3,1,4,2,0:T(8,128)S(1)} %fusion.60) | copy-start | bytes 14155780
  118.3 7.4 %copy-start.8 = (bf16[2,384,2048]{2,1,0:T(8,128)(2,1)S(1)}, bf16[2,384,2048]{2,1,0:T(8,128)(2,1)}, u32[]{:S(2)}) copy-start(bf16[2,384,2048]{2,1,0:T(8,128)(2,1)} %param.12) | copy-start | bytes 9437188
  196.4 88.8 %all-to-all-start.2 = ((bf16[128,24,1024]{2,1,0:T(8,128)(2,1)}), bf16[128,24,1024]{2,1,0:T(8,128)(2,1)}, u32[]{:S(2)}, u32[]{:S(2)}) async-start(bf16[128,24,1024]{2,1,0:T(8,128)(2,1)} %bitcast.215), calls=%async_computation.2 | async-start | bytes 12582912 | tf_op jit(solution)/shard_map/all_to_all | solution.py:73
  216.8 21.0 %slice-start.2 = ((s8[6291456]{0:T(1024)(128)(4,1)}), s8[2097152]{0:T(1024)(128)(4,1)S(1)}, s32[]{:S(2)}) async-start(s8[6291456]{0:T(1024)(128)(4,1)} %bitcast.227), calls=%async_computation.6 | async-start | bytes 4194304
  221.6 16.2 %slice-start.3 = ((s8[6291456]{0:T(1024)(128)(4,1)}), s8[4194304]{0:T(1024)(128)(4,1)S(1)}, s32[]{:S(2)}) async-start(s8[6291456]{0:T(1024)(128)(4,1)} %bitcast.227), calls=%async_computation.7 | async-start | bytes 8388608
  236.4 1.4 copy-start.14
  244.3 5.2 %copy-start.15 = (bf16[64,24,2,384]{3,1,2,0:T(8,128)(2,1)S(1)}, bf16[64,24,2,384]{3,1,2,0:T(8,128)(2,1)}, u32[]{:S(2)}) copy-start(bf16[64,24,2,384]{3,1,2,0:T(8,128)(2,1)} %copy-done.14) | copy-start | bytes 7077892
  249.5 4.3 %copy-start.10 = (bf16[2,2048,384]{2,1,0:T(8,128)(2,1)S(1)}, bf16[2,2048,384]{2,1,0:T(8,128)(2,1)}, u32[]{:S(2)}) copy-start(bf16[2,2048,384]{2,1,0:T(8,128)(2,1)} %param.10) | copy-start | bytes 9437188
  249.5 4.3 %copy-start.16 = (bf16[64,24,2,384]{3,1,2,0:T(8,128)(2,1)S(1)}, bf16[64,24,2,384]{3,1,2,0:T(8,128)(2,1)}, u32[]{:S(2)}) copy-start(bf16[64,24,2,384]{3,1,2,0:T(8,128)(2,1)} %copy-done.14) | copy-start | bytes 7077892
  253.8 2.8 copy-start.12
  253.8 2.7 copy-start.13
  285.2 89.3 %all-to-all-start.3 = ((bf16[128,24,1024]{2,1,0:T(8,128)(2,1)}), bf16[128,24,1024]{2,1,0:T(8,128)(2,1)}, u32[]{:S(2)}, u32[]{:S(2)}) async-start(bf16[128,24,1024]{2,1,0:T(8,128)(2,1)} %bitcast.213), calls=%async_computation.3 | async-start | bytes 12582912 | tf_op jit(solution)/shard_map/all_to_all | solution.py:73
  301.0 4.7 %copy-start.6 = (bf16[128,1024]{1,0:T(8,128)(2,1)S(1)}, bf16[128,1024]{1,0:T(8,128)(2,1)}, u32[]{:S(2)}) copy-start(bf16[128,1024]{1,0:T(8,128)(2,1)} %param.13) | copy-start | bytes 786436
  312.6 5.5 %copy-start.4 = (s32[128,8]{1,0:T(8,128)S(1)}, s32[128,8]{1,0:T(8,128)}, u32[]{:S(2)}) copy-start(s32[128,8]{1,0:T(8,128)} %copy-done.3) | copy-start | bytes 12292
  312.6 61.9 %copy-start.2 = (bf16[128,1536]{0,1:T(8,128)(2,1)S(1)}, bf16[128,1536]{0,1:T(8,128)(2,1)}, u32[]{:S(2)}) copy-start(bf16[128,1536]{0,1:T(8,128)(2,1)} %copy.80) | copy-start | bytes 1179652
  374.6 4.6 %copy-start.1 = (bf16[128,2048]{1,0:T(8,128)(2,1)S(1)}, bf16[128,2048]{1,0:T(8,128)(2,1)}, u32[]{:S(2)}) copy-start(bf16[128,2048]{1,0:T(8,128)(2,1)} %param.7) | copy-start | bytes 1572868
